TPU v7x, 256 devices: a whole 4x4x8 slice. The times are simulated.
256 devices in a mesh: dp: 128 (over y, z, x), rep: 2 (over core).
Axes of the slice: x: 4, y: 4, z: 8, core: 2. Of those that a mesh axis runs over, the one named last changes fastest.
Arguments:
- embeddings: float32 [131072, 1024], P(('dp', 'rep')), may hold values from -6 to 6
- cluster_ids: int32 [131072, 1], P(('dp', 'rep')), may hold values from 0 to 255; in each aligned block of 512 rows (0 to 511, 512 to 1023, ...) at most 4 rows name the same one
- boundary_slots: int32 [256, 2, 256], P(('dp', 'rep')), may hold values from 0 to 1023
Outputs:
- member_max: float32 [256, 1024], P(('dp', 'rep'))
- centrality: float32 [256, 1024], P(('dp', 'rep'))
Inputs may be any that keep to these rules, and one draw needn't show every extreme that they name: `cluster_ids`: among the rows of one device, at most 4 name the same cluster, a bound that some block reaches of them; every cluster is named by some row.
All inputs are finite; a program needn't handle non-finite values.
Results may differ from a plain program's by a relative error of at most 0.0024.
Values may be sent and summed in bfloat16 or wider, within the bound.
A program may use at most 64 MiB of HBM per device.

v0:
```python
import jax
import jax.numpy as jnp
from jax import lax
from jax.sharding import PartitionSpec as P

SLOTS = 1024
eps = 1e-06


def from_behind(array, axis, by):
    peers = lax.axis_size(axis)
    pairs = [(i, i + by) for i in range(peers) if 0 <= i + by < peers]
    return lax.ppermute(array, axis, pairs)


def per_device(embeddings, cluster_ids, boundary_slots):
    n_chips = lax.axis_size("dp")
    n_cores = lax.axis_size("rep")
    owners = n_chips * n_cores
    width = embeddings.shape[1]
    slots = SLOTS
    capacity = slots // owners
    bound = boundary_slots.shape[2]
    me = lax.axis_index(("dp", "rep"))
    labels = cluster_ids[:, 0]
    member_of = labels[:, None] == jnp.arange(owners, dtype=jnp.int32)[None, :]
    running = jnp.cumsum(member_of.astype(jnp.int32), axis=0)
    ranks = jnp.sum(jnp.where(member_of, running, 0), axis=1) - 1
    targets = labels * capacity + ranks
    unit_full = embeddings * lax.rsqrt(
        jnp.sum(embeddings * embeddings, axis=1, keepdims=True) + eps
    )
    unit_half = unit_full.astype(jnp.bfloat16)
    outgoing = jnp.zeros((slots, width), jnp.bfloat16).at[targets].set(unit_half)
    shaped = outgoing.reshape(n_chips, n_cores, capacity, width)
    arrived = lax.all_to_all(
        lax.all_to_all(shaped, "dp", split_axis=0, concat_axis=0, tiled=True),
        "rep",
        split_axis=1,
        concat_axis=1,
        tiled=True,
    )
    members = arrived.reshape(slots, width)
    own_sum = lax.dot_general(
        jnp.ones((1, slots), jnp.bfloat16),
        members,
        (((1,), (0,)), ((), ())),
        preferred_element_type=jnp.float32,
    )
    direction = own_sum[0] * lax.rsqrt(jnp.sum(own_sum * own_sum) + eps)
    lengths = jnp.einsum("se,se->s", members, members, preferred_element_type=jnp.float32)
    filled = lengths > 0.5
    filled_int = filled.astype(jnp.int32)
    count = jnp.sum(filled_int)
    order = jnp.argsort(1 - filled_int, stable=True)
    picks = boundary_slots[0] % count
    positions = order[picks.reshape(-1)]
    outward = members[positions]
    lower = from_behind(outward[bound:], ("dp", "rep"), 1)
    upper = from_behind(outward[:bound], ("dp", "rep"), -1)
    candidates = jnp.concatenate([members, lower, upper], axis=0)
    cand_ok = jnp.concatenate(
        [filled, jnp.full((bound,), me > 0), jnp.full((bound,), me < owners - 1)]
    )
    column = jnp.arange(slots + 2 * bound, dtype=jnp.int32)
    block = min(512, slots)

    def one_block(start):
        block_rows = lax.dynamic_slice_in_dim(members, start, block, 0)
        scores = lax.dot_general(
            block_rows, candidates, (((1,), (1,)), ((), ())), preferred_element_type=jnp.float32
        )
        row_pos = start + jnp.arange(block, dtype=jnp.int32)
        keep = cand_ok[None, :] & (column[None, :] != row_pos[:, None])
        return jnp.max(jnp.where(keep, scores, -1.0), axis=1)

    starts = jnp.arange(slots // block, dtype=jnp.int32) * block
    best = lax.map(one_block, starts).reshape(slots)
    member_max = jnp.where(filled, best, 0.0)
    central = jnp.dot(
        members, direction, precision=lax.Precision.HIGHEST, preferred_element_type=jnp.float32
    )
    centrality = jnp.where(filled, central, 0.0)
    return (member_max[None, :], centrality[None, :])


def solution(mesh):
    placed = (P(("dp", "rep"), None), P(("dp", "rep"), None), P(("dp", "rep"), None, None))
    return jax.shard_map(
        per_device,
        mesh=mesh,
        in_specs=placed,
        out_specs=(P(("dp", "rep"), None), P(("dp", "rep"), None)),
        check_vma=False,
    )
```

profile of v0, /device:TPU:7, one launch (start us, length us, event | category | flops | bytes accessed | tf_op | source)
XLA Modules:
  0.0 137.3 jit_solution(18101900111716776001)
XLA Ops:
  0.6 0.0 copy-start.1
  0.6 0.0 copy-start
  0.6 0.9 copy.12
  1.6 0.2 fusion.11
  1.9 0.1 copy.13
  2.0 0.0 copy-done.1
  2.0 0.2 fusion.10
  2.3 0.0 copy-done
  2.3 0.2 multiply_reduce_fusion
  2.5 4.2 %scatter_custom_fusion = bf16[1024,1024]{1,0:T(8,128)(2,1)} fusion(s32[512]{0:T(512)S(1)} %bitcast.60, f32[512,1024]{1,0:T(8,128)S(1)} %copy-done, f32[512]{0:T(512)S(1)} %add_rsqrt_fusion, bf16[]{:T(256)} %constant.27.clone.1), kind=kCustom, calls=%fused_computation.16 | custom fusion | flops 1048576 | bytes 4196354 | tf_op jit(solution)/shard_map/scatter | solution.py:34
  6.7 2.7 %reshape.111 = bf16[128,2,4,1024]{3,2,1,0:T(4,128)(2,1)S(1)} reshape(bf16[1024,1024]{1,0:T(8,128)(2,1)} %scatter_custom_fusion) | data formatting | bytes 4194304 | tf_op jit(solution)/shard_map/reshape | solution.py:35
  9.5 64.2 %all_to_all.10 = bf16[128,2,4,1024]{3,2,1,0:T(4,128)(2,1)S(1)} all-to-all(bf16[128,2,4,1024]{3,2,1,0:T(4,128)(2,1)S(1)} %reshape.111), channel_id=1, replica_groups=mesh['dp'=128,'rep'=2] {'dp'}, dimensions={0} | all-to-all | bytes 4194304 | tf_op jit(solution)/shard_map/all_to_all | solution.py:37
  73.6 0.7 copy.14
  74.4 8.0 %all_to_all.11 = bf16[128,2,4,1024]{3,2,0,1:T(4,128)(2,1)S(1)} all-to-all(bf16[128,2,4,1024]{3,2,0,1:T(4,128)(2,1)S(1)} %copy.14), channel_id=1, replica_groups=mesh['dp'=128,'rep'=2] {'rep'}, dimensions={1} | all-to-all | bytes 4194304 | tf_op jit(solution)/shard_map/all_to_all | solution.py:36
  82.3 2.6 %copy.15 = bf16[128,2,4,1024]{3,2,1,0:T(4,128)(2,1)} copy(bf16[128,2,4,1024]{3,2,0,1:T(4,128)(2,1)S(1)} %all_to_all.11) | data formatting | bytes 4194304 | tf_op jit(solution)/shard_map/all_to_all | solution.py:36
  85.0 2.5 %reshape.112 = bf16[1024,1024]{1,0:T(8,128)(2,1)S(1)} reshape(bf16[128,2,4,1024]{3,2,1,0:T(4,128)(2,1)} %copy.15) | data formatting | bytes 4194304 | tf_op jit(solution)/shard_map/reshape | solution.py:43
  87.5 0.4 fusion.14
  87.9 0.0 copy-start.2
  87.9 0.5 fusion.6
  88.4 0.6 multiply_reduce_fusion.1
  89.7 1.7 %fusion.18 = f32[1,1024]{1,0:T(1,128)S(1)} fusion(bf16[1024,1024]{1,0:T(8,128)(2,1)S(1)} %reshape.112, f32[1024,1]{0,1:T(1,128)S(1)} %bitcast.50), kind=kOutput, calls=%fused_computation.50 | convolution fusion | flops 12582912 | bytes 2105344 | tf_op jit(solution)/shard_map/dot_general | solution.py:80
  91.4 0.6 broadcast_select_fusion
  92.0 0.6 convert_reduce_fusion
  93.9 0.0 copy-done.2
  93.9 0.1 remainder_bitcast_fusion
  94.1 4.4 %sort.17 = (s32[1024]{0:T(1024)}, s32[1024]{0:T(1024)S(1)}) sort(s32[1024]{0:T(1024)S(1)} %get-tuple-element.73, s32[1024]{0:T(1024)S(1)} %iota.25), dimensions={0}, to_apply=%region_5.6 | sort | flops 10240 | bytes 16384 | tf_op jit(solution)/shard_map/jit(argsort)/sort | solution.py:55
  98.5 2.3 %gather_fusion = s32[512]{0:T(512)S(1)} fusion(s32[1024]{0:T(1024)S(1)} %get-tuple-element.40, s32[1024]{0:T(1024)S(1)} %pad_clamp_fusion.1), kind=kCustom, calls=%fused_computation | custom fusion | bytes 6144 | tf_op jit(solution)/shard_map/gather | solution.py:57
  100.8 2.1 %gather_fusion.1 = bf16[512,1024]{1,0:T(8,128)(2,1)S(1)} fusion(bf16[1024,1024]{1,0:T(8,128)(2,1)S(1)} %reshape.112, s32[1024]{0:T(1024)S(1)} %pad_clamp_fusion), kind=kCustom, calls=%fused_computation.1 | custom fusion | bytes 2099200 | tf_op jit(solution)/shard_map/gather | solution.py:58
  102.9 1.1 fusion.17
  103.9 4.4 %collective-permute-start = (bf16[256,1024]{1,0:T(8,128)(2,1)}, bf16[256,1024]{1,0:T(8,128)(2,1)S(1)}, u32[]{:S(2)}, u32[]{:S(2)}) collective-permute-start(bf16[256,1024]{1,0:T(8,128)(2,1)} %get-tuple-element.70), channel_id=1, source_target_pairs={{0,1},{1,2},{2,3},{3,4},{4,5},{5,6},{6,7},{7,8},{8,9},{9,10},{10,1... | collective-permute-start | bytes 1572872 | tf_op jit(solution)/shard_map/ppermute | solution.py:13
  108.3 1.9 %collective-permute-start.1 = (bf16[256,1024]{1,0:T(8,128)(2,1)}, bf16[256,1024]{1,0:T(8,128)(2,1)S(1)}, u32[]{:S(2)}, u32[]{:S(2)}) collective-permute-start(bf16[256,1024]{1,0:T(8,128)(2,1)} %get-tuple-element.71), channel_id=1, source_target_pairs={{1,0},{2,1},{3,2},{4,3},{5,4},{6,5},{7,6},{8,7},{9,8},{10,9},{11,1... | collective-permute-start | bytes 1572872 | tf_op jit(solution)/shard_map/ppermute | solution.py:13
  110.3 4.4 %collective-permute-done = bf16[256,1024]{1,0:T(8,128)(2,1)S(1)} collective-permute-done((bf16[256,1024]{1,0:T(8,128)(2,1)}, bf16[256,1024]{1,0:T(8,128)(2,1)S(1)}, u32[]{:S(2)}, u32[]{:S(2)}) %collective-permute-start) | collective-permute-done | bytes 524320 | tf_op jit(solution)/shard_map/ppermute | solution.py:13
  114.8 6.4 %collective-permute-done.1 = bf16[256,1024]{1,0:T(8,128)(2,1)S(1)} collective-permute-done((bf16[256,1024]{1,0:T(8,128)(2,1)}, bf16[256,1024]{1,0:T(8,128)(2,1)S(1)}, u32[]{:S(2)}, u32[]{:S(2)}) %collective-permute-start.1) | collective-permute-done | bytes 524320 | tf_op jit(solution)/shard_map/ppermute | solution.py:13
  121.2 1.9 %pad_maximum_fusion = bf16[1536,1024]{1,0:T(8,128)(2,1)} fusion(bf16[256,1024]{1,0:T(8,128)(2,1)S(1)} %collective-permute-done.1, bf16[256,1024]{1,0:T(8,128)(2,1)S(1)} %collective-permute-done, bf16[1024,1024]{1,0:T(8,128)(2,1)S(1)} %reshape.112), kind=kLoop, calls=%fused_computation.13 | loop fusion | flops 9437184 | bytes 6291456 | tf_op jit(solution)/shard_map/concatenate | solution.py:61
  123.1 13.6 %while.11 = (s32[]{:T(128)}, f32[2,512]{1,0:T(2,128)S(1)}, pred[1536]{0:T(1024)(128)(4,1)S(1)}, s32[2]{0:T(128)S(1)}, bf16[1024,1024]{1,0:T(8,128)(2,1)S(1)}, /*...) while((s32[]{:T(128)}, f32[2,512]{1,0:T(2,128)S(1)}, ...), condition=%wide.region_9.10_spmd.clone, body=%wide.region_7.9_spmd.clone.sunk | while | flops 1613758464 | bytes 4206743 | solution.py:78
  123.1 0.5 dynamic_slice.14
  125.2 0.5 iota_add_fusion.2
  125.8 4.0 %fusion.28 = f32[512]{0:T(512)S(1)} fusion(bf16[1536,1024]{1,0:T(8,128)(2,1)} %get-tuple-element.134, s32[512]{0:T(512)S(1)} %iota_add_fusion.2, pred[1536]{0:T(1024)(128)(4,1)S(1)} %get-tuple-element.131, bf16[1024,1024]{1,0:T(8,128)(2,1)S(1)} %get-tuple-element.133, s32[]{:T(128)S(6)} %select_n.86), kind=kOutput, calls=%fused_computation.7.clone.1 | convolution fusion | flops 1613757952 | bytes 4200452 | tf_op jit(solution)/shard_map/while/body/eval_jaxpr/dot_general | solution.py:70
  129.9 0.6 dynamic_slice.14
  132.0 0.5 iota_add_fusion.2
  132.6 4.0 %fusion.28 = f32[512]{0:T(512)S(1)} fusion(bf16[1536,1024]{1,0:T(8,128)(2,1)} %get-tuple-element.134, s32[512]{0:T(512)S(1)} %iota_add_fusion.2, pred[1536]{0:T(1024)(128)(4,1)S(1)} %get-tuple-element.131, bf16[1024,1024]{1,0:T(8,128)(2,1)S(1)} %get-tuple-element.133, s32[]{:T(128)S(6)} %select_n.86), kind=kOutput, calls=%fused_computation.7.clone.1 | convolution fusion | flops 1613757952 | bytes 4200452 | tf_op jit(solution)/shard_map/while/body/eval_jaxpr/dot_general | solution.py:70
  136.7 0.6 broadcast_select_fusion.1
  (23 shorter events, 0.3 us)
Async XLA Ops:
  0.6 1.4 %copy-start.1 = (s32[512,1]{0,1:T(1,128)S(1)}, s32[512,1]{0,1:T(1,128)}, u32[]{:S(2)}) copy-start(s32[512,1]{0,1:T(1,128)} %param.6) | copy-start | bytes 6148
  0.6 1.6 %copy-start = (f32[512,1024]{1,0:T(8,128)S(1)}, f32[512,1024]{1,0:T(8,128)}, u32[]{:S(2)}) copy-start(f32[512,1024]{1,0:T(8,128)} %param.5) | copy-start | bytes 6291460
  87.9 6.1 %copy-start.2 = (s32[1,2,256]{2,1,0:T(2,128)S(1)}, s32[1,2,256]{2,1,0:T(2,128)}, u32[]{:S(2)}) copy-start(s32[1,2,256]{2,1,0:T(2,128)} %param.7) | copy-start | bytes 6148
  103.9 10.8 %collective-permute-start = (bf16[256,1024]{1,0:T(8,128)(2,1)}, bf16[256,1024]{1,0:T(8,128)(2,1)S(1)}, u32[]{:S(2)}, u32[]{:S(2)}) collective-permute-start(bf16[256,1024]{1,0:T(8,128)(2,1)} %get-tuple-element.70), channel_id=1, source_target_pairs={{0,1},{1,2},{2,3},{3,4},{4,5},{5,6},{6,7},{7,8},{8,9},{9,10},{10,1... | collective-permute-start | bytes 1572872 | tf_op jit(solution)/shard_map/ppermute | solution.py:13
  108.3 12.8 %collective-permute-start.1 = (bf16[256,1024]{1,0:T(8,128)(2,1)}, bf16[256,1024]{1,0:T(8,128)(2,1)S(1)}, u32[]{:S(2)}, u32[]{:S(2)}) collective-permute-start(bf16[256,1024]{1,0:T(8,128)(2,1)} %get-tuple-element.71), channel_id=1, source_target_pairs={{1,0},{2,1},{3,2},{4,3},{5,4},{6,5},{7,6},{8,7},{9,8},{10,9},{11,1... | collective-permute-start | bytes 1572872 | tf_op jit(solution)/shard_map/ppermute | solution.py:13
where the time goes:
time: 138 us; the launch traced here: 137 us
  blocking collectives  72.1 us (52%)
  local copies, waits for them, and re-layouts  16.3 us (12%)
  other arithmetic  15.4 us (11%)
  waiting for transfers between devices  10.8 us (8%)
  matrix products  10.1 us (7%)
  starting transfers between devices  6.31 us (5%)
  loops' own time  3.3 us (2%)
  between operations  2.89 us (2%)
    all_to_all x1, blocking collectives, per_device(): lax.all_to_all(shaped, 'dp', split_axis=0, concat_axis=0, tiled=True)  64.2 us
    ppermute x2, waiting for transfers between devices, from_behind(): return lax.ppermute(array, axis, pairs)  10.8 us
    dot_general x2, matrix products, one_block(): lax.dot_general(block_rows, candidates, (((1,), (1,)), ((), ())), preferr...  8.02 us
    all_to_all x1, blocking collectives, per_device(): lax.all_to_all(lax.all_to_all(shaped, 'dp', split_axis=0, concat_axis=0,...  7.97 us
    ppermute x2, starting transfers between devices, from_behind(): return lax.ppermute(array, axis, pairs)  6.31 us
    sort x1, other arithmetic, per_device(): order = jnp.argsort(1 - filled_int, stable=True)  4.37 us
    scatter x1, other arithmetic, per_device(): jnp.zeros((slots, width), jnp.bfloat16).at[targets].set(unit_half)  4.22 us
    another operation x1, loops' own time, per_device(): best = lax.map(one_block, starts).reshape(slots)  3.3 us
  transfers between devices with their start and end apart: 2, of which 2 were waited for; matrix products, arithmetic and copies ran while one was open for 0% of the time, Pallas kernels for 0%

commit v1 on v0

--- a/solution.py
+++ b/solution.py
@@ -33,12 +33,20 @@
     unit_half = unit_full.astype(jnp.bfloat16)
     outgoing = jnp.zeros((slots, width), jnp.bfloat16).at[targets].set(unit_half)
     shaped = outgoing.reshape(n_chips, n_cores, capacity, width)
-    arrived = lax.all_to_all(
-        lax.all_to_all(shaped, "dp", split_axis=0, concat_axis=0, tiled=True),
-        "rep",
-        split_axis=1,
-        concat_axis=1,
-        tiled=True,
+    arrived = jnp.concatenate(
+        lax.all_to_all(
+            jnp.stack(
+                jnp.split(
+                    lax.all_to_all(shaped, "dp", split_axis=0, concat_axis=0, tiled=True),
+                    lax.axis_size("rep"),
+                    axis=1,
+                )
+            ),
+            "rep",
+            0,
+            0,
+        ),
+        axis=1,
     )
     members = arrived.reshape(slots, width)
     own_sum = lax.dot_general(

time: 138 us -> 139 us (level)
  other arithmetic: 15.4 us -> 16.9 us
    all_to_all x2 -> x0, local copies, waits for them, and re-layouts: 3.35 us -> none  [the longest x1 2.63 us: per_device(): lax.all_to_all(lax.all_to_all(shaped, 'dp', split_axis=0, concat_axis=0,...]
    another operation x3 -> x5, local copies, waits for them, and re-layouts: 0.11 us -> 3.37 us  [the longest x1 2.54 us: per_device(): members = arrived.reshape(slots, width)]
    another operation x3 -> x4, other arithmetic: 0.27 us -> 1.76 us  [the longest x1 1.48 us: per_device(): jnp.stack(jnp.split(lax.all_to_all(shaped, 'dp', split_axis=0, concat_axi...]
where the time goes in v1:
time: 139 us
  blocking collectives  72.2 us (52%)
  other arithmetic  16.9 us (12%)
  local copies, waits for them, and re-layouts  16.3 us (12%)
  waiting for transfers between devices  10.8 us (8%)
  matrix products  10.1 us (7%)
  starting transfers between devices  6.26 us (5%)
  loops' own time  3.3 us (2%)
  between operations  2.9 us (2%)
    all_to_all x1, blocking collectives, per_device(): lax.all_to_all(shaped, 'dp', split_axis=0, concat_axis=0, tiled=True)  64.2 us
    ppermute x2, waiting for transfers between devices, from_behind(): return lax.ppermute(array, axis, pairs)  10.8 us
    all_to_all x1, blocking collectives, per_device(): lax.all_to_all(jnp.stack(jnp.split(lax.all_to_all(shaped, 'dp', split_axi...  8.02 us
    dot_general x2, matrix products, one_block(): lax.dot_general(block_rows, candidates, (((1,), (1,)), ((), ())), preferr...  8.02 us
    ppermute x2, starting transfers between devices, from_behind(): return lax.ppermute(array, axis, pairs)  6.26 us
    sort x1, other arithmetic, per_device(): order = jnp.argsort(1 - filled_int, stable=True)  4.37 us
    scatter x1, other arithmetic, per_device(): jnp.zeros((slots, width), jnp.bfloat16).at[targets].set(unit_half)  4.22 us
    another operation x1, loops' own time, per_device(): best = lax.map(one_block, starts).reshape(slots)  3.3 us
  transfers between devices with their start and end apart: 2, of which 2 were waited for; matrix products, arithmetic and copies ran while one was open for 0% of the time, Pallas kernels for 0%

profile of v1, /device:TPU:7, one launch (start us, length us, event | category | flops | bytes accessed | tf_op | source)
XLA Modules:
  0.0 138.8 jit_solution(4149091080611865029)
XLA Ops:
  0.6 0.0 copy-start.1
  0.6 0.0 copy-start
  0.6 0.9 copy.7
  1.6 0.2 fusion.11
  1.9 0.1 copy.8
  2.0 0.0 copy-done.1
  2.0 0.2 fusion.10
  2.3 0.0 copy-done
  2.3 0.2 multiply_reduce_fusion
  2.5 4.2 %scatter_custom_fusion = bf16[1024,1024]{1,0:T(8,128)(2,1)} fusion(s32[512]{0:T(512)S(1)} %bitcast.70, f32[512,1024]{1,0:T(8,128)S(1)} %copy-done, f32[512]{0:T(512)S(1)} %add_rsqrt_fusion, bf16[]{:T(256)} %constant.27.clone.1), kind=kCustom, calls=%fused_computation.17 | custom fusion | flops 1048576 | bytes 4196354 | tf_op jit(solution)/shard_map/scatter | solution.py:34
  6.7 2.7 %reshape.111 = bf16[128,2,4,1024]{3,2,1,0:T(4,128)(2,1)S(1)} reshape(bf16[1024,1024]{1,0:T(8,128)(2,1)} %scatter_custom_fusion) | data formatting | bytes 4194304 | tf_op jit(solution)/shard_map/reshape | solution.py:35
  9.5 64.2 %all_to_all.10 = bf16[128,2,4,1024]{3,2,1,0:T(4,128)(2,1)S(1)} all-to-all(bf16[128,2,4,1024]{3,2,1,0:T(4,128)(2,1)S(1)} %reshape.111), channel_id=1, replica_groups=mesh['dp'=128,'rep'=2] {'dp'}, dimensions={0} | all-to-all | bytes 4194304 | tf_op jit(solution)/shard_map/all_to_all | solution.py:40
  73.6 0.7 slice_bitcast_fusion.1
  74.4 1.5 %pad_maximum_fusion.1 = bf16[2,128,1,4,1024]{4,3,1,2,0:T(4,128)(2,1)S(1)} fusion(bf16[1,128,1,4,1024]{4,3,1,2,0:T(4,128)(2,1)S(1)} %get-tuple-element.71, bf16[1,128,1,4,1024]{4,3,1,2,0:T(4,128)(2,1)S(1)} %get-tuple-element.70), kind=kLoop, calls=%fused_computation.14 | loop fusion | flops 1048576 | bytes 4194304 | tf_op jit(solution)/shard_map/stack | solution.py:38
  75.8 8.0 %all_to_all.11 = bf16[2,128,1,4,1024]{4,3,1,2,0:T(4,128)(2,1)S(1)} all-to-all(bf16[2,128,1,4,1024]{4,3,1,2,0:T(4,128)(2,1)S(1)} %pad_maximum_fusion.1), channel_id=1, replica_groups=mesh['dp'=128,'rep'=2] {'rep'}, dimensions={0} | all-to-all | bytes 4194304 | tf_op jit(solution)/shard_map/all_to_all | solution.py:37
  83.9 2.6 %copy.10 = bf16[128,2,1,4,1024]{4,3,1,0,2:T(4,128)(2,1)} copy(bf16[128,2,1,4,1024]{4,3,0,2,1:T(4,128)(2,1)S(1)} %bitcast.50) | data formatting | bytes 4194304 | tf_op jit(solution)/shard_map/reshape | solution.py:36
  86.5 2.5 %reshape_reshape.3 = bf16[1024,1024]{1,0:T(8,128)(2,1)S(1)} reshape(bf16[128,2,1,4,1024]{4,3,1,0,2:T(4,128)(2,1)} %copy.10) | data formatting | bytes 4194304 | tf_op jit(solution)/shard_map/reshape;reshape | solution.py:51
  89.0 0.4 fusion.14
  89.4 0.0 copy-start.2
  89.4 0.5 fusion.6
  89.9 0.6 multiply_reduce_fusion.1
  91.2 1.7 %fusion.18 = f32[1,1024]{1,0:T(1,128)S(1)} fusion(bf16[1024,1024]{1,0:T(8,128)(2,1)S(1)} %reshape_reshape.3, f32[1024,1]{0,1:T(1,128)S(1)} %bitcast.60), kind=kOutput, calls=%fused_computation.53 | convolution fusion | flops 12582912 | bytes 2105344 | tf_op jit(solution)/shard_map/dot_general | solution.py:88
  92.9 0.6 broadcast_select_fusion
  93.6 0.6 convert_reduce_fusion
  95.5 0.0 copy-done.2
  95.5 0.1 remainder_bitcast_fusion
  95.7 4.4 %sort.17 = (s32[1024]{0:T(1024)}, s32[1024]{0:T(1024)S(1)}) sort(s32[1024]{0:T(1024)S(1)} %get-tuple-element.75, s32[1024]{0:T(1024)S(1)} %iota.25), dimensions={0}, to_apply=%region_5.6 | sort | flops 10240 | bytes 16384 | tf_op jit(solution)/shard_map/jit(argsort)/sort | solution.py:63
  100.0 2.3 %gather_fusion = s32[512]{0:T(512)S(1)} fusion(s32[1024]{0:T(1024)S(1)} %get-tuple-element.40, s32[1024]{0:T(1024)S(1)} %pad_clamp_fusion.1), kind=kCustom, calls=%fused_computation | custom fusion | bytes 6144 | tf_op jit(solution)/shard_map/gather | solution.py:65
  102.4 2.1 %gather_fusion.1 = bf16[512,1024]{1,0:T(8,128)(2,1)S(1)} fusion(bf16[1024,1024]{1,0:T(8,128)(2,1)S(1)} %reshape_reshape.3, s32[1024]{0:T(1024)S(1)} %pad_clamp_fusion), kind=kCustom, calls=%fused_computation.1 | custom fusion | bytes 2099200 | tf_op jit(solution)/shard_map/gather | solution.py:66
  104.4 1.1 fusion.17
  105.5 4.3 %collective-permute-start = (bf16[256,1024]{1,0:T(8,128)(2,1)}, bf16[256,1024]{1,0:T(8,128)(2,1)S(1)}, u32[]{:S(2)}, u32[]{:S(2)}) collective-permute-start(bf16[256,1024]{1,0:T(8,128)(2,1)} %get-tuple-element.72), channel_id=1, source_target_pairs={{0,1},{1,2},{2,3},{3,4},{4,5},{5,6},{6,7},{7,8},{8,9},{9,10},{10,1... | collective-permute-start | bytes 1572872 | tf_op jit(solution)/shard_map/ppermute | solution.py:13
  109.8 1.9 %collective-permute-start.1 = (bf16[256,1024]{1,0:T(8,128)(2,1)}, bf16[256,1024]{1,0:T(8,128)(2,1)S(1)}, u32[]{:S(2)}, u32[]{:S(2)}) collective-permute-start(bf16[256,1024]{1,0:T(8,128)(2,1)} %get-tuple-element.73), channel_id=1, source_target_pairs={{1,0},{2,1},{3,2},{4,3},{5,4},{6,5},{7,6},{8,7},{9,8},{10,9},{11,1... | collective-permute-start | bytes 1572872 | tf_op jit(solution)/shard_map/ppermute | solution.py:13
  111.8 4.4 %collective-permute-done = bf16[256,1024]{1,0:T(8,128)(2,1)S(1)} collective-permute-done((bf16[256,1024]{1,0:T(8,128)(2,1)}, bf16[256,1024]{1,0:T(8,128)(2,1)S(1)}, u32[]{:S(2)}, u32[]{:S(2)}) %collective-permute-start) | collective-permute-done | bytes 524320 | tf_op jit(solution)/shard_map/ppermute | solution.py:13
  116.2 6.4 %collective-permute-done.1 = bf16[256,1024]{1,0:T(8,128)(2,1)S(1)} collective-permute-done((bf16[256,1024]{1,0:T(8,128)(2,1)}, bf16[256,1024]{1,0:T(8,128)(2,1)S(1)}, u32[]{:S(2)}, u32[]{:S(2)}) %collective-permute-start.1) | collective-permute-done | bytes 524320 | tf_op jit(solution)/shard_map/ppermute | solution.py:13
  122.6 1.9 %pad_maximum_fusion = bf16[1536,1024]{1,0:T(8,128)(2,1)} fusion(bf16[256,1024]{1,0:T(8,128)(2,1)S(1)} %collective-permute-done.1, bf16[256,1024]{1,0:T(8,128)(2,1)S(1)} %collective-permute-done, bf16[1024,1024]{1,0:T(8,128)(2,1)S(1)} %reshape_reshape.3), kind=kLoop, calls=%fused_computation.13 | loop fusion | flops 9437184 | bytes 6291456 | tf_op jit(solution)/shard_map/concatenate | solution.py:69
  124.5 13.6 %while.11 = (s32[]{:T(128)}, f32[2,512]{1,0:T(2,128)S(1)}, pred[1536]{0:T(1024)(128)(4,1)S(1)}, s32[2]{0:T(128)S(1)}, bf16[1024,1024]{1,0:T(8,128)(2,1)S(1)}, /*...) while((s32[]{:T(128)}, f32[2,512]{1,0:T(2,128)S(1)}, ...), condition=%wide.region_9.10_spmd.clone, body=%wide.region_7.9_spmd.clone.sunk | while | flops 1613758464 | bytes 4206743 | solution.py:86
  124.5 0.5 dynamic_slice.14
  126.7 0.5 iota_add_fusion.2
  127.3 4.0 %fusion.28 = f32[512]{0:T(512)S(1)} fusion(bf16[1536,1024]{1,0:T(8,128)(2,1)} %get-tuple-element.136, s32[512]{0:T(512)S(1)} %iota_add_fusion.2, pred[1536]{0:T(1024)(128)(4,1)S(1)} %get-tuple-element.133, bf16[1024,1024]{1,0:T(8,128)(2,1)S(1)} %get-tuple-element.135, s32[]{:T(128)S(6)} %select_n.86), kind=kOutput, calls=%fused_computation.7.clone.1 | convolution fusion | flops 1613757952 | bytes 4200452 | tf_op jit(solution)/shard_map/while/body/eval_jaxpr/dot_general | solution.py:78
  131.3 0.6 dynamic_slice.14
  133.5 0.5 iota_add_fusion.2
  134.1 4.0 %fusion.28 = f32[512]{0:T(512)S(1)} fusion(bf16[1536,1024]{1,0:T(8,128)(2,1)} %get-tuple-element.136, s32[512]{0:T(512)S(1)} %iota_add_fusion.2, pred[1536]{0:T(1024)(128)(4,1)S(1)} %get-tuple-element.133, bf16[1024,1024]{1,0:T(8,128)(2,1)S(1)} %get-tuple-element.135, s32[]{:T(128)S(6)} %select_n.86), kind=kOutput, calls=%fused_computation.7.clone.1 | convolution fusion | flops 1613757952 | bytes 4200452 | tf_op jit(solution)/shard_map/while/body/eval_jaxpr/dot_general | solution.py:78
  138.2 0.6 broadcast_select_fusion.1
  (23 shorter events, 0.3 us)
Async XLA Ops:
  0.6 1.4 copy-start.1
  0.6 1.6 %copy-start = (f32[512,1024]{1,0:T(8,128)S(1)}, f32[512,1024]{1,0:T(8,128)}, u32[]{:S(2)}) copy-start(f32[512,1024]{1,0:T(8,128)} %param.5) | copy-start | bytes 6291460
  89.4 6.1 %copy-start.2 = (s32[1,2,256]{2,1,0:T(2,128)S(1)}, s32[1,2,256]{2,1,0:T(2,128)}, u32[]{:S(2)}) copy-start(s32[1,2,256]{2,1,0:T(2,128)} %param.7) | copy-start | bytes 6148
  105.5 10.8 %collective-permute-start = (bf16[256,1024]{1,0:T(8,128)(2,1)}, bf16[256,1024]{1,0:T(8,128)(2,1)S(1)}, u32[]{:S(2)}, u32[]{:S(2)}) collective-permute-start(bf16[256,1024]{1,0:T(8,128)(2,1)} %get-tuple-element.72), channel_id=1, source_target_pairs={{0,1},{1,2},{2,3},{3,4},{4,5},{5,6},{6,7},{7,8},{8,9},{9,10},{10,1... | collective-permute-start | bytes 1572872 | tf_op jit(solution)/shard_map/ppermute | solution.py:13
  109.8 12.8 %collective-permute-start.1 = (bf16[256,1024]{1,0:T(8,128)(2,1)}, bf16[256,1024]{1,0:T(8,128)(2,1)S(1)}, u32[]{:S(2)}, u32[]{:S(2)}) collective-permute-start(bf16[256,1024]{1,0:T(8,128)(2,1)} %get-tuple-element.73), channel_id=1, source_target_pairs={{1,0},{2,1},{3,2},{4,3},{5,4},{6,5},{7,6},{8,7},{9,8},{10,9},{11,1... | collective-permute-start | bytes 1572872 | tf_op jit(solution)/shard_map/ppermute | solution.py:13
